TPU v7x, 32 devices: a whole 2x2x4 slice. The times are simulated.
32 devices in a mesh: fsdp: 2 (over y), ctx: 16 (over z, x, core).
Axes of the slice: x: 2, y: 2, z: 4, core: 2. Of those that a mesh axis runs over, the one named last changes fastest.
Arguments:
- layer_input: bfloat16 [8, 1024, 1024], P('fsdp', 'ctx'), may hold values from -6 to 6
- output_grad: bfloat16 [8, 1024, 1024], P('fsdp', 'ctx'), may hold values from -6 to 6
- segments: int32 [8, 1024], P('fsdp'), may hold values from 0 to 3, never falling along the last dimension, each value on 1 to 512 neighbouring positions
- assignment: int32 [16], replicated, may hold values from 0 to 15, each once
- first_gain: bfloat16 [1024], P('fsdp'), may hold values from 0.5 to 1.5
- first_bias: bfloat16 [1024], P('fsdp'), may hold values from -1.5 to 1.5
- input_weight: bfloat16 [1024, 3072], P('fsdp'), may hold values from -0.25 to 0.25
- query_bias: bfloat16 [1024], P('fsdp'), may hold values from -2.5 to 2.5
- value_bias: bfloat16 [1024], P('fsdp'), may hold values from -2.5 to 2.5
- output_weight: bfloat16 [1024, 1024], P(None, 'fsdp'), may hold values from -1.5 to 1.5
- output_bias: bfloat16 [1024], P('fsdp'), may hold values from -1.5 to 1.5
- second_gain: bfloat16 [1024], P('fsdp'), may hold values from 0.5 to 1.5
- second_bias: bfloat16 [1024], P('fsdp'), may hold values from -1.5 to 1.5
- expand_weight: bfloat16 [1024, 4096], P('fsdp'), may hold values from -0.1875 to 0.1875
- expand_bias: bfloat16 [4096], P('fsdp'), may hold values from -2.5 to 2.5
- shrink_weight: bfloat16 [4096, 1024], P(None, 'fsdp'), may hold values from -0.09375 to 0.09375
- shrink_bias: bfloat16 [1024], P('fsdp'), may hold values from -1.5 to 1.5
Outputs:
- layer_output: bfloat16 [8, 1024, 1024], P('fsdp', 'ctx')
- input_grad: float32 [8, 1024, 1024], P('fsdp', 'ctx')
- first_gain_grad: float32 [1024], P('fsdp')
- first_bias_grad: float32 [1024], P('fsdp')
- input_weight_grad: float32 [1024, 3072], P('fsdp')
- query_bias_grad: float32 [1024], P('fsdp')
- value_bias_grad: float32 [1024], P('fsdp')
- output_weight_grad: float32 [1024, 1024], P(None, 'fsdp')
- output_bias_grad: float32 [1024], P('fsdp')
- second_gain_grad: float32 [1024], P('fsdp')
- second_bias_grad: float32 [1024], P('fsdp')
- expand_weight_grad: float32 [1024, 4096], P('fsdp')
- expand_bias_grad: float32 [4096], P('fsdp')
- shrink_weight_grad: float32 [4096, 1024], P(None, 'fsdp')
- shrink_bias_grad: float32 [1024], P('fsdp')
Inputs may be any that keep to these rules, and one draw needn't show every extreme that they name: `segments`: in each sequence, in the order of positions, the document numbers never fall; each document has 1 to 512 positions and one has exactly 512. A permutation: index i of ctx holds the blocks assignment[i] and 31 - assignment[i] of every sequence.
All inputs are finite; a program needn't handle non-finite values.
Results may differ from a plain program's by a relative error of at most 0.012.
The roundings to bfloat16 on the way count: a program that leaves them out, or rounds other values in their place, can miss the bound.
Values may be sent and summed in bfloat16 or wider, within the bound.
No kernel may reach another device: no remote copies, remote signals or barrier semaphores. Data moves between devices by JAX's collectives and lax.ppermute only.
A program may use at most 320 MiB of HBM per device.

v0:
```python
import math
import jax
import jax.numpy as jnp
from jax import lax
from jax.sharding import PartitionSpec as P

HEADS = 16
MICRO = 2
EPSILON = 1e-05
MASKED = -1000000000.0


def layer_norm(inputs, norm_gain, norm_bias):
    center = inputs - jnp.mean(inputs, axis=-1, keepdims=True)
    spread = jnp.mean(center * center, axis=-1, keepdims=True)
    return center * lax.rsqrt(spread + EPSILON) * norm_gain + norm_bias


def gelu_tanh(inputs):
    return jax.nn.gelu(inputs, approximate=True)


def key_places(assignment, row_count, length):
    pairs = assignment.shape[0]
    span_len = row_count // 2
    places = jnp.arange(length, dtype=jnp.int32)
    owner = places // row_count
    within = places % row_count
    match = owner[:, None] == jnp.arange(pairs, dtype=jnp.int32)[None, :]
    paired = jnp.sum(jnp.where(match, assignment[None, :], 0), axis=1)
    early = paired * span_len + within
    later = (2 * pairs - 1 - paired) * span_len + within - span_len
    return jnp.where(within < span_len, early, later)


def masked_scores(queries, key_rows, query_place, key_place, query_doc, key_doc, inv_root):
    scores = (
        jnp.einsum("sqhd,skhd->shqk", queries, key_rows, preferred_element_type=jnp.float32)
        * inv_root
    )
    allowed = (key_place[None, None, :] <= query_place[None, :, None]) & (
        key_doc[:, None, :] == query_doc[:, :, None]
    )
    return jnp.where(allowed[:, None], scores, MASKED)


def one_batch(weights, layer_input, output_grad, segments, places, own_places):
    (
        first_gain,
        first_bias,
        input_weight,
        query_bias,
        value_bias,
        output_weight,
        output_bias,
        second_gain,
        second_bias,
        expand_weight,
        expand_bias,
        shrink_weight,
        shrink_bias,
    ) = weights
    seq_count, row_count, features = layer_input.shape
    head_count = HEADS
    head_size = features // head_count
    inv_root = 1.0 / math.sqrt(head_size)
    length = places.shape[0]
    size_k = min(512, length)
    blocks = length // size_k
    key_docs = jnp.take(segments, places, axis=1)
    own_docs = jnp.take(segments, own_places, axis=1)
    inputs = layer_input.astype(jnp.float32)
    normed, first_pull = jax.vjp(
        layer_norm, inputs, first_gain.astype(jnp.float32), first_bias.astype(jnp.float32)
    )
    normed = normed.astype(jnp.bfloat16)
    joined = jnp.einsum("srd,de->sre", normed, input_weight, preferred_element_type=jnp.float32)
    queries = (joined[..., :features] + query_bias.astype(jnp.float32)).astype(jnp.bfloat16)
    key_value = jnp.concatenate(
        [
            joined[..., features : 2 * features],
            joined[..., 2 * features :] + value_bias.astype(jnp.float32),
        ],
        axis=-1,
    ).astype(jnp.bfloat16)
    gathered = lax.all_gather(key_value, "ctx", axis=1, tiled=True)
    query_heads = queries.reshape(seq_count, row_count, head_count, head_size)

    def key_block(number):
        offset = number * size_k
        pieces = lax.dynamic_slice_in_dim(gathered, offset, size_k, 1)
        key_rows = pieces[..., :features].reshape(seq_count, size_k, head_count, head_size)
        value_rows = pieces[..., features:].reshape(seq_count, size_k, head_count, head_size)
        block_places = lax.dynamic_slice_in_dim(places, offset, size_k, 0)
        block_docs = lax.dynamic_slice_in_dim(key_docs, offset, size_k, 1)
        scores = masked_scores(
            query_heads, key_rows, own_places, block_places, own_docs, block_docs, inv_root
        )
        return (key_rows, value_rows, scores)

    def max_sum(number, running):
        scores = key_block(number)[2]
        highest = jnp.maximum(running[0], jnp.max(scores, axis=-1))
        totals = running[1] * jnp.exp(running[0] - highest) + jnp.sum(
            jnp.exp(scores - highest[..., None]), axis=-1
        )
        return (highest, totals)

    stats_shape = (seq_count, head_count, row_count)
    highest, totals = lax.fori_loop(
        0,
        blocks,
        max_sum,
        (jnp.full(stats_shape, MASKED, jnp.float32), jnp.zeros(stats_shape, jnp.float32)),
    )
    log_total = highest + jnp.log(totals)

    def mix_values(number, running):
        pieces = key_block(number)
        probs_low = jnp.exp(pieces[2] - log_total[..., None]).astype(jnp.bfloat16)
        return running + jnp.einsum(
            "shqk,skhd->sqhd", probs_low, pieces[1], preferred_element_type=jnp.float32
        )

    mixed_heads = lax.fori_loop(
        0, blocks, mix_values, jnp.zeros((seq_count, row_count, head_count, head_size), jnp.float32)
    )
    mixed_low = mixed_heads.reshape(seq_count, row_count, features).astype(jnp.bfloat16)
    residual = (
        inputs
        + jnp.einsum("sre,ed->srd", mixed_low, output_weight, preferred_element_type=jnp.float32)
        + output_bias.astype(jnp.float32)
    )
    normed_two, second_pull = jax.vjp(
        layer_norm, residual, second_gain.astype(jnp.float32), second_bias.astype(jnp.float32)
    )
    normed_two = normed_two.astype(jnp.bfloat16)
    hidden = jnp.einsum(
        "srd,df->srf", normed_two, expand_weight, preferred_element_type=jnp.float32
    ) + expand_bias.astype(jnp.float32)
    active, gelu_pull = jax.vjp(gelu_tanh, hidden)
    active = active.astype(jnp.bfloat16)
    layer_output = (
        residual
        + jnp.einsum("srf,fd->srd", active, shrink_weight, preferred_element_type=jnp.float32)
        + shrink_bias.astype(jnp.float32)
    ).astype(jnp.bfloat16)
    cotangent = output_grad.astype(jnp.float32)
    shrink_weight_grad = jnp.einsum(
        "srf,srd->fd", active, output_grad, preferred_element_type=jnp.float32
    )
    shrink_bias_grad = jnp.sum(cotangent, axis=(0, 1))
    hidden_grad = gelu_pull(
        jnp.einsum("srd,fd->srf", output_grad, shrink_weight, preferred_element_type=jnp.float32)
    )[0].astype(jnp.bfloat16)
    expand_weight_grad = jnp.einsum(
        "srd,srf->df", normed_two, hidden_grad, preferred_element_type=jnp.float32
    )
    expand_bias_grad = jnp.sum(hidden_grad.astype(jnp.float32), axis=(0, 1))
    second_grads = second_pull(
        jnp.einsum("srf,df->srd", hidden_grad, expand_weight, preferred_element_type=jnp.float32)
    )
    residual_grad = cotangent + second_grads[0]
    branch_grad = residual_grad.astype(jnp.bfloat16)
    output_weight_grad = jnp.einsum(
        "sre,srd->ed", mixed_low, branch_grad, preferred_element_type=jnp.float32
    )
    output_bias_grad = jnp.sum(branch_grad.astype(jnp.float32), axis=(0, 1))
    mixed_flat = jnp.einsum(
        "srd,ed->sre", branch_grad, output_weight, preferred_element_type=jnp.float32
    ).astype(jnp.bfloat16)
    mixed_grad = mixed_flat.reshape(seq_count, row_count, head_count, head_size)

    def prob_grads(pieces):
        probs = jnp.exp(pieces[2] - log_total[..., None])
        prob_grad = jnp.einsum(
            "sqhd,skhd->shqk", mixed_grad, pieces[1], preferred_element_type=jnp.float32
        )
        return (probs, prob_grad)

    def delta_sum(number, running):
        probs, prob_grad = prob_grads(key_block(number))
        return running + jnp.sum(probs * prob_grad, axis=-1)

    deltas = lax.fori_loop(0, blocks, delta_sum, jnp.zeros(stats_shape, jnp.float32))
    query_zero = jnp.zeros((seq_count, row_count, head_count, head_size), jnp.float32)

    def key_grads(number, running):
        pieces = key_block(number)
        probs, prob_grad = prob_grads(pieces)
        score_grad = (probs * (prob_grad - deltas[..., None])).astype(jnp.bfloat16)
        query_grad = (
            running[0]
            + jnp.einsum(
                "shqk,skhd->sqhd", score_grad, pieces[0], preferred_element_type=jnp.float32
            )
            * inv_root
        )
        key_grad = (
            jnp.einsum(
                "shqk,sqhd->skhd", score_grad, query_heads, preferred_element_type=jnp.float32
            )
            * inv_root
        )
        value_grad = jnp.einsum(
            "shqk,sqhd->skhd",
            probs.astype(jnp.bfloat16),
            mixed_grad,
            preferred_element_type=jnp.float32,
        )
        joined_grad = jnp.concatenate(
            [
                key_grad.reshape(seq_count, size_k, features),
                value_grad.reshape(seq_count, size_k, features),
            ],
            axis=-1,
        )
        buffer = lax.dynamic_update_slice_in_dim(running[1], joined_grad, number * size_k, 1)
        return (query_grad, buffer)

    query_grad, buffer = lax.fori_loop(
        0,
        blocks,
        key_grads,
        (query_zero, jnp.zeros((seq_count, length, 2 * features), jnp.float32)),
    )
    key_value_grad = lax.psum_scatter(buffer, "ctx", scatter_dimension=1, tiled=True).astype(
        jnp.bfloat16
    )
    query_low = query_grad.reshape(seq_count, row_count, features).astype(jnp.bfloat16)
    joined_low = jnp.concatenate([query_low, key_value_grad], axis=-1)
    input_weight_grad = jnp.einsum(
        "srd,sre->de", normed, joined_low, preferred_element_type=jnp.float32
    )
    query_bias_grad = jnp.sum(query_low.astype(jnp.float32), axis=(0, 1))
    value_bias_grad = jnp.sum(key_value_grad[..., features:].astype(jnp.float32), axis=(0, 1))
    first_grads = first_pull(
        jnp.einsum("sre,de->srd", joined_low, input_weight, preferred_element_type=jnp.float32)
    )
    input_grad = residual_grad + first_grads[0]
    grads = (
        first_grads[1],
        first_grads[2],
        input_weight_grad,
        query_bias_grad,
        value_bias_grad,
        output_weight_grad,
        output_bias_grad,
        second_grads[1],
        second_grads[2],
        expand_weight_grad,
        expand_bias_grad,
        shrink_weight_grad,
        shrink_bias_grad,
    )
    return (layer_output, input_grad, grads)


def body(
    layer_input,
    output_grad,
    segments,
    assignment,
    first_gain,
    first_bias,
    input_weight,
    query_bias,
    value_bias,
    output_weight,
    output_bias,
    second_gain,
    second_bias,
    expand_weight,
    expand_bias,
    shrink_weight,
    shrink_bias,
):
    row_count = layer_input.shape[1]
    length = row_count * lax.axis_size("ctx")
    places = key_places(assignment, row_count, length)
    own_places = lax.dynamic_slice_in_dim(places, lax.axis_index("ctx") * row_count, row_count, 0)
    batch_seqs = layer_input.shape[0] // MICRO
    outputs = []
    input_grads = []
    summed = None
    for micro_turn in range(MICRO):
        weights = (
            lax.all_gather(first_gain, "fsdp", axis=0, tiled=True),
            lax.all_gather(first_bias, "fsdp", axis=0, tiled=True),
            lax.all_gather(input_weight, "fsdp", axis=0, tiled=True),
            lax.all_gather(query_bias, "fsdp", axis=0, tiled=True),
            lax.all_gather(value_bias, "fsdp", axis=0, tiled=True),
            lax.all_gather(output_weight, "fsdp", axis=1, tiled=True),
            lax.all_gather(output_bias, "fsdp", axis=0, tiled=True),
            lax.all_gather(second_gain, "fsdp", axis=0, tiled=True),
            lax.all_gather(second_bias, "fsdp", axis=0, tiled=True),
            lax.all_gather(expand_weight, "fsdp", axis=0, tiled=True),
            lax.all_gather(expand_bias, "fsdp", axis=0, tiled=True),
            lax.all_gather(shrink_weight, "fsdp", axis=1, tiled=True),
            lax.all_gather(shrink_bias, "fsdp", axis=0, tiled=True),
        )
        lower = micro_turn * batch_seqs
        upper = lower + batch_seqs
        result = one_batch(
            weights,
            layer_input[lower:upper],
            output_grad[lower:upper],
            segments[lower:upper],
            places,
            own_places,
        )
        outputs.append(result[0])
        input_grads.append(result[1])
        batch_grads = result[2]
        summed = (
            batch_grads
            if summed is None
            else tuple((first + second for first, second in zip(summed, batch_grads)))
        )
    summed = lax.psum(
        (
            lax.psum_scatter(summed[0], "fsdp", scatter_dimension=0, tiled=True),
            lax.psum_scatter(summed[1], "fsdp", scatter_dimension=0, tiled=True),
            lax.psum_scatter(summed[2], "fsdp", scatter_dimension=0, tiled=True),
            lax.psum_scatter(summed[3], "fsdp", scatter_dimension=0, tiled=True),
            lax.psum_scatter(summed[4], "fsdp", scatter_dimension=0, tiled=True),
            lax.psum_scatter(summed[5], "fsdp", scatter_dimension=1, tiled=True),
            lax.psum_scatter(summed[6], "fsdp", scatter_dimension=0, tiled=True),
            lax.psum_scatter(summed[7], "fsdp", scatter_dimension=0, tiled=True),
            lax.psum_scatter(summed[8], "fsdp", scatter_dimension=0, tiled=True),
            lax.psum_scatter(summed[9], "fsdp", scatter_dimension=0, tiled=True),
            lax.psum_scatter(summed[10], "fsdp", scatter_dimension=0, tiled=True),
            lax.psum_scatter(summed[11], "fsdp", scatter_dimension=1, tiled=True),
            lax.psum_scatter(summed[12], "fsdp", scatter_dimension=0, tiled=True),
        ),
        "ctx",
    )
    return (
        jnp.concatenate(outputs, axis=0),
        jnp.concatenate(input_grads, axis=0),
        summed[0],
        summed[1],
        summed[2],
        summed[3],
        summed[4],
        summed[5],
        summed[6],
        summed[7],
        summed[8],
        summed[9],
        summed[10],
        summed[11],
        summed[12],
    )


def solution(mesh):
    return jax.shard_map(
        body,
        mesh=mesh,
        in_specs=(
            P("fsdp", "ctx", None),
            P("fsdp", "ctx", None),
            P("fsdp", None),
            P(),
            P("fsdp"),
            P("fsdp"),
            P("fsdp", None),
            P("fsdp"),
            P("fsdp"),
            P(None, "fsdp"),
            P("fsdp"),
            P("fsdp"),
            P("fsdp"),
            P("fsdp", None),
            P("fsdp"),
            P(None, "fsdp"),
            P("fsdp"),
        ),
        out_specs=(
            P("fsdp", "ctx", None),
            P("fsdp", "ctx", None),
            P("fsdp"),
            P("fsdp"),
            P("fsdp", None),
            P("fsdp"),
            P("fsdp"),
            P(None, "fsdp"),
            P("fsdp"),
            P("fsdp"),
            P("fsdp"),
            P("fsdp", None),
            P("fsdp"),
            P(None, "fsdp"),
            P("fsdp"),
        ),
        check_vma=False,
    )
```

profile of v0, /device:TPU:0, one launch (start us, length us, event | category | flops | bytes accessed | tf_op | source)
XLA Modules:
  0.0 2027.5 jit_solution(2020608010366841230)
XLA Ops:
  27.5 65.3 %all-gather.15.cloned.1.call-done = bf16[1024,3072]{1,0:T(8,128)(2,1)} async-done(((bf16[512,3072]{1,0:T(8,128)(2,1)}), bf16[1024,3072]{1,0:T(8,128)(2,1)}) %all-gather.15.cloned.1.call-update) | async-done | bytes 6291472 | tf_op jit(solution)/shard_map/all_gather | solution.py:290
  131.0 43.7 %all-gather.25.cloned.1.call-done = bf16[2,1024,2048]{2,1,0:T(8,128)(2,1)} async-done(((bf16[2,64,2048]{2,1,0:T(8,128)(2,1)}), bf16[2,1024,2048]{2,1,0:T(8,128)(2,1)}) %all-gather.25.cloned.1.call-update) | async-done | bytes 8388624 | tf_op jit(solution)/shard_map/all_gather | solution.py:86
  174.7 12.0 copy.147
  186.6 16.3 while.122
  203.0 17.4 while.123
  222.4 28.2 %all-gather.17.cloned.1.call-done = bf16[2,1024,2048]{2,1,0:T(8,128)(2,1)} async-done(((bf16[2,64,2048]{2,1,0:T(8,128)(2,1)}), bf16[2,1024,2048]{2,1,0:T(8,128)(2,1)}) %all-gather.17.cloned.1.call-update) | async-done | bytes 8388624 | tf_op jit(solution)/shard_map/all_gather | solution.py:86
  250.6 12.0 copy.137
  262.6 16.3 while.120
  278.9 18.0 while.121
  303.5 85.4 %all-gather.21.cloned.1.call-done = bf16[1024,4096]{1,0:T(8,128)(2,1)} async-done(((bf16[512,4096]{1,0:T(8,128)(2,1)}), bf16[1024,4096]{1,0:T(8,128)(2,1)}) %all-gather.21.cloned.1.call-update) | async-done | bytes 8388624 | tf_op jit(solution)/shard_map/all_gather | solution.py:297
  397.9 96.4 %all-gather.23.cloned.1.call-done = bf16[4096,1024]{1,0:T(8,128)(2,1)} async-done(((bf16[4096,512]{1,0:T(8,128)(2,1)}), bf16[4096,1024]{1,0:T(8,128)(2,1)}) %all-gather.23.cloned.1.call-update) | async-done | bytes 8388624 | tf_op jit(solution)/shard_map/all_gather | solution.py:299
  523.0 10.5 while.126
  541.4 66.1 %while.127 = (s32[]{:T(128)}, f32[2,64,16,64]{1,3,2,0:T(8,128)}, f32[2,1024,2048]{2,1,0:T(8,128)}, bf16[2,1024,2048]{1,2,0:T(8,128)(2,1)}, s32[1024]{0:T(1024)S(...) while((s32[]{:T(128)}, f32[2,64,16,64]{1,3,2,0:T(8,128)}, ...), condition=%wide.region_37.40_spmd.clone, body=%wide.region_36.39_spmd.clone.sunk | while | flops 685277184 | bytes 136621136 | solution.py:221
  612.6 11.8 while.124
  624.5 10.5 broadcast.727.clone2.1
  635.0 66.7 %while.125 = (s32[]{:T(128)}, f32[2,64,16,64]{1,3,2,0:T(8,128)}, f32[2,1024,2048]{2,1,0:T(8,128)}, bf16[2,1024,2048]{1,2,0:T(8,128)(2,1)}, s32[1024]{0:T(1024)S(...) while((s32[]{:T(128)}, f32[2,64,16,64]{1,3,2,0:T(8,128)}, ...), condition=%wide.region_27.30_spmd.clone, body=%wide.region_26.29_spmd.clone.sunk | while | flops 685277184 | bytes 136621136 | solution.py:221
  737.3 48.9 %reduce-scatter.9.cloned.1.call-done = f32[2,64,2048]{2,1,0:T(8,128)} async-done(((f32[2,1024,2048]{2,1,0:T(8,128)}), f32[2,64,2048]{2,1,0:T(8,128)}) %reduce-scatter.9.cloned.1.call-update) | async-done | bytes 1048592 | tf_op jit(solution)/shard_map/reduce_scatter | solution.py:227
  787.5 180.4 %reduce-scatter.7.cloned.1.call-done = f32[2,64,2048]{2,1,0:T(8,128)} async-done(((f32[2,1024,2048]{2,1,0:T(8,128)}), f32[2,64,2048]{2,1,0:T(8,128)}) %reduce-scatter.7.cloned.1.call-update) | async-done | bytes 1048592 | tf_op jit(solution)/shard_map/reduce_scatter | solution.py:227
  978.1 46.0 %reduce-scatter.13.cloned.1.call-done = f32[1024,512]{1,0:T(8,128)} async-done(((f32[1024,1024]{1,0:T(8,128)}), f32[1024,512]{1,0:T(8,128)}) %reduce-scatter.13.cloned.1.call-update) | async-done | bytes 2097168 | tf_op jit(solution)/shard_map/reduce_scatter | solution.py:327
  1024.2 191.4 %reduce-scatter.15.cloned.1.call-done = f32[512,4096]{1,0:T(8,128)} async-done(((f32[1024,4096]{1,0:T(8,128)}), f32[512,4096]{1,0:T(8,128)}) %reduce-scatter.15.cloned.1.call-update) | async-done | bytes 8388624 | tf_op jit(solution)/shard_map/reduce_scatter | solution.py:331
  1215.6 191.5 %reduce-scatter.17.cloned.1.call-done = f32[4096,512]{1,0:T(8,128)} async-done(((f32[4096,1024]{1,0:T(8,128)}), f32[4096,512]{1,0:T(8,128)}) %reduce-scatter.17.cloned.1.call-update) | async-done | bytes 8388624 | tf_op jit(solution)/shard_map/reduce_scatter | solution.py:333
  1407.0 146.8 %reduce-scatter.11.cloned.1.call-done = f32[512,3072]{1,0:T(8,128)} async-done(((f32[1024,3072]{1,0:T(8,128)}), f32[512,3072]{1,0:T(8,128)}) %reduce-scatter.11.cloned.1.call-update) | async-done | bytes 6291472 | tf_op jit(solution)/shard_map/reduce_scatter | solution.py:324
  1587.2 63.6 %all-reduce.9 = (f32[512]{0:T(512)}, f32[512]{0:T(512)}, f32[512]{0:T(512)}, f32[512]{0:T(512)}, f32[512]{0:T(512)}, /*index=5*/f32[512]{0:T(512)}, f32[512]{0:T(512)}, f32[2048]{0:T(1024)}, f32[512]{0:T(512)}) all-reduce(f32[512]{0:T(512)S(1)} %dynamic-slice.1, ...), channel_id=1, replica_groups=mesh['fsdp'=2,'ctx'=16] {'ctx'}, use_global_device_ids=true, to_apply=%region_44.47 | all-reduce | flops 6144 | bytes 49152 | tf_op jit(solution)/shard_map/psum | solution.py:320
  1652.4 350.5 %all-reduce.14.cloned.1.call-done = (f32[512,3072]{1,0:T(8,128)}, f32[1024,512]{1,0:T(8,128)}, f32[512,4096]{1,0:T(8,128)}, f32[4096,512]{1,0:T(8,128)}) async-done(((f32[512,3072]{1,0:T(8,128)}, f32[1024,512]{1,0:T(8,128)}, f32[512,4096]{1,0:T(8,128)}, f32[4096,512]{1,0:T(8,128)}), (f32[512,3072]{1,0:T(8,128)}, f32[1024,512]{1,0:T(8,128)}, f32[512,4096]{1,0:T(8,128)}, ...) | async-done | bytes 25165840 | tf_op jit(solution)/shard_map/psum | solution.py:320
  (582 shorter events, 436.0 us)
Async XLA Ops:
  7.2 85.5 %all-gather.15.cloned.1.call-start = ((), (), s32[]{:S(2)}) async-start(), calls=%async_computation.6 | async-start | bytes 9437184 | tf_op jit(solution)/shard_map/all_gather | solution.py:290
  8.0 166.7 %all-gather.25.cloned.1.call-start = ((), (), s32[]{:S(2)}) async-start(), calls=%async_computation.11 | async-start | bytes 8912896 | tf_op jit(solution)/shard_map/all_gather | solution.py:86
  99.6 151.1 %all-gather.17.cloned.1.call-start = ((), (), s32[]{:S(2)}) async-start(), calls=%async_computation.7 | async-start | bytes 8912896 | tf_op jit(solution)/shard_map/all_gather | solution.py:86
  100.5 198.8 %all-gather.19.cloned.1.call-start = ((), (), s32[]{:S(2)}) async-start(), calls=%async_computation.8 | async-start | bytes 3145728 | tf_op jit(solution)/shard_map/all_gather | solution.py:293
  101.1 287.8 %all-gather.21.cloned.1.call-start = ((), (), s32[]{:S(2)}) async-start(), calls=%async_computation.9 | async-start | bytes 12582912 | tf_op jit(solution)/shard_map/all_gather | solution.py:297
  101.7 392.6 %all-gather.23.cloned.1.call-start = ((), (), s32[]{:S(2)}) async-start(), calls=%async_computation.10 | async-start | bytes 12582912 | tf_op jit(solution)/shard_map/all_gather | solution.py:299
  102.3 683.9 %reduce-scatter.9.cloned.1.call-start = ((), (), s32[]{:S(2)}) async-start(), calls=%async_computation.13 | async-start | bytes 17825792 | tf_op jit(solution)/shard_map/reduce_scatter | solution.py:227
  123.6 271.6 %copy-start.55 = (f32[2,1,512]{2,1,0:T(1,128)}, f32[2,1,512]{2,1,0:T(1,128)S(1)}, u32[]{:S(2)}) copy-start(f32[2,1,512]{2,1,0:T(1,128)S(1)} %convert_element_type.251) | copy-start | bytes 12292
  128.5 389.8 %copy-start.50 = (f32[2,1,512]{2,1,0:T(1,128)}, f32[2,1,512]{2,1,0:T(1,128)S(1)}, u32[]{:S(2)}) copy-start(f32[2,1,512]{2,1,0:T(1,128)S(1)} %convert_element_type.250) | copy-start | bytes 12292
  302.1 216.1 %copy-start.63 = (f32[2,64]{1,0:T(2,128)}, f32[2,64]{1,0:T(2,128)S(1)}, u32[]{:S(2)}) copy-start(f32[2,64]{1,0:T(2,128)S(1)} %broadcast_multiply_fusion) | copy-start | bytes 1540
  303.2 215.1 %copy-start.20 = (f32[2,64,1024]{2,1,0:T(8,128)}, f32[2,64,1024]{2,1,0:T(8,128)S(1)}, u32[]{:S(2)}) copy-start(f32[2,64,1024]{2,1,0:T(8,128)S(1)} %get-tuple-element.2151) | copy-start | bytes 1572868
  607.5 360.4 %reduce-scatter.7.cloned.1.call-start = ((), (), s32[]{:S(2)}) async-start(), calls=%async_computation.12 | async-start | bytes 17825792 | tf_op jit(solution)/shard_map/reduce_scatter | solution.py:227
  701.8 322.4 %reduce-scatter.13.cloned.1.call-start = ((), (), s32[]{:S(2)}) async-start(), calls=%async_computation.15 | async-start | bytes 6291456 | tf_op jit(solution)/shard_map/reduce_scatter | solution.py:327
  706.5 509.1 %reduce-scatter.15.cloned.1.call-start = ((), (), s32[]{:S(2)}) async-start(), calls=%async_computation.16 | async-start | bytes 25165824 | tf_op jit(solution)/shard_map/reduce_scatter | solution.py:331
  718.6 688.4 %reduce-scatter.17.cloned.1.call-start = ((), (), s32[]{:S(2)}) async-start(), calls=%async_computation.17 | async-start | bytes 25165824 | tf_op jit(solution)/shard_map/reduce_scatter | solution.py:333
  733.5 820.3 %reduce-scatter.11.cloned.1.call-start = ((), (), s32[]{:S(2)}) async-start(), calls=%async_computation.14 | async-start | bytes 18874368 | tf_op jit(solution)/shard_map/reduce_scatter | solution.py:324
  737.0 232.2 %copy-start.16 = (bf16[4,64,1024]{2,1,0:T(8,128)(2,1)S(1)}, bf16[4,64,1024]{2,1,0:T(8,128)(2,1)}, u32[]{:S(2)}) copy-start(bf16[4,64,1024]{2,1,0:T(8,128)(2,1)} %param.37) | copy-start | bytes 1572868
  737.0 232.2 %copy-start.49 = (f32[2,1,512]{2,1,0:T(1,128)S(1)}, f32[2,1,512]{2,1,0:T(1,128)}, u32[]{:S(2)}) copy-start(f32[2,1,512]{2,1,0:T(1,128)} %copy-done.48) | copy-start | bytes 12292
  737.1 232.2 %copy-start.54 = (f32[2,1,512]{2,1,0:T(1,128)S(1)}, f32[2,1,512]{2,1,0:T(1,128)}, u32[]{:S(2)}) copy-start(f32[2,1,512]{2,1,0:T(1,128)} %copy-done.53) | copy-start | bytes 12292
  737.1 232.2 %copy-start.70 = (f32[2,64]{1,0:T(2,128)S(1)}, f32[2,64]{1,0:T(2,128)}, u32[]{:S(2)}) copy-start(f32[2,64]{1,0:T(2,128)} %copy-done.69) | copy-start | bytes 1540
  737.1 232.2 %copy-start.76 = (f32[2,64]{1,0:T(2,128)S(1)}, f32[2,64]{1,0:T(2,128)}, u32[]{:S(2)}) copy-start(f32[2,64]{1,0:T(2,128)} %copy-done.75) | copy-start | bytes 1540
  787.5 785.4 %copy-start.41 = (bf16[2,64,2048]{2,1,0:T(8,128)(2,1)}, bf16[2,64,2048]{2,1,0:T(8,128)(2,1)S(1)}, u32[]{:S(2)}) copy-start(bf16[2,64,2048]{2,1,0:T(8,128)(2,1)S(1)} %convert_element_type.236) | copy-start | bytes 1572868
  969.3 605.8 %copy-start.43 = (bf16[2,64,2048]{2,1,0:T(8,128)(2,1)}, bf16[2,64,2048]{2,1,0:T(8,128)(2,1)S(1)}, u32[]{:S(2)}) copy-start(bf16[2,64,2048]{2,1,0:T(8,128)(2,1)S(1)} %convert_element_type.229) | copy-start | bytes 1572868
  978.1 1024.9 %all-reduce.14.cloned.1.call-start = ((), (), s32[]{:S(2)}) async-start(), calls=%async_computation.18 | async-start | bytes 50331648 | tf_op jit(solution)/shard_map/psum | solution.py:320
  (111 other events, 2029.4 us)
Sparse Core Ops, SparseCore 0:
  9.6 83.0 all-gather.14
  99.7 74.9 all-gather.24
  177.4 73.1 all-gather.16
  252.0 31.3 all-gather.18
  284.8 103.9 all-gather.20
  390.2 103.9 all-gather.22
  607.7 178.5 reduce-scatter.8
  790.3 177.5 reduce-scatter.6
  970.8 53.3 reduce-scatter.12
  1026.4 189.1 reduce-scatter.14
  1217.9 189.1 reduce-scatter.16
  1409.3 144.4 reduce-scatter.10
  1559.5 443.4 all-reduce.13
where the time goes:
time: 2030 us
  waiting for transfers between devices  1480 us (73%)
  local copies, waits for them, and re-layouts  198 us (10%)
  matrix products  171 us (8%)
  blocking collectives  111 us (5%)
  other arithmetic  51.2 us (3%)
    psum x1, waiting for transfers between devices, body(): lax.psum((lax.psum_scatter(summed[0], 'fsdp', scatter_dimension=0, tiled=...  351 us
    reduce_scatter x2, waiting for transfers between devices, one_batch(): lax.psum_scatter(buffer, 'ctx', scatter_dimension=1, tiled=True)  229 us
    reduce_scatter x1, waiting for transfers between devices, body(): lax.psum_scatter(summed[11], 'fsdp', scatter_dimension=1, tiled=True)  191 us
    reduce_scatter x1, waiting for transfers between devices, body(): lax.psum_scatter(summed[9], 'fsdp', scatter_dimension=0, tiled=True)  191 us
    reduce_scatter x1, waiting for transfers between devices, body(): lax.psum_scatter(summed[2], 'fsdp', scatter_dimension=0, tiled=True)  147 us
    all_gather x1, waiting for transfers between devices, body(): lax.all_gather(shrink_weight, 'fsdp', axis=1, tiled=True)  96.4 us
    all_gather x1, waiting for transfers between devices, body(): lax.all_gather(expand_weight, 'fsdp', axis=0, tiled=True)  85.4 us
    all_gather x2, waiting for transfers between devices, one_batch(): gathered = lax.all_gather(key_value, 'ctx', axis=1, tiled=True)  71.8 us
  transfers between devices with their start and end apart: 13, of which 12 were waited for; matrix products, arithmetic and copies ran while one was open for 14% of the time, Pallas kernels for 0%

commit v1 on v0

--- a/solution.py
+++ b/solution.py
@@ -83,7 +83,12 @@
         ],
         axis=-1,
     ).astype(jnp.bfloat16)
-    gathered = lax.all_gather(key_value, "ctx", axis=1, tiled=True)
+    ring = [key_value]
+    for hop in range(15):
+        ring.append(lax.ppermute(ring[-1], "ctx", [(dev, (dev + 1) % 16) for dev in range(16)]))
+    gathered = jnp.roll(
+        jnp.concatenate(ring[::-1], axis=1), (lax.axis_index("ctx") + 1) * ring[0].shape[1], axis=1
+    )
     query_heads = queries.reshape(seq_count, row_count, head_count, head_size)
 
     def key_block(number):

time: 2030 us -> 1970 us (0.970)
  waiting for transfers between devices: 1480 us -> 1370 us
    ppermute x0 -> x30, waiting for transfers between devices: none -> 156 us  [one_batch(): lax.ppermute(ring[-1], 'ctx', [(dev, (dev + 1) % 16) for dev in range(16)])]
    all_gather x1, waiting for transfers between devices: 96.4 us -> 0.01 us  [body(): lax.all_gather(shrink_weight, 'fsdp', axis=1, tiled=True)]
    all_gather x1, waiting for transfers between devices: 85.4 us -> 0.02 us  [body(): lax.all_gather(expand_weight, 'fsdp', axis=0, tiled=True)]
    all_gather x2 -> x0, waiting for transfers between devices: 71.8 us -> none  [one_batch(): gathered = lax.all_gather(key_value, 'ctx', axis=1, tiled=True)]
    unnamed x258 -> x388, local copies, waits for them, and re-layouts: 56.1 us -> 74.9 us
  transfers between devices with their start and end apart: 13 -> 41, of which waited for: 12 -> 36; matrix products, arithmetic and copies ran while one was open for 14% -> 16% of each run, Pallas kernels for 0% -> 0%
where the time goes in v1:
time: 1970 us; the launch traced here: 1960 us
  waiting for transfers between devices  1370 us (70%)
  local copies, waits for them, and re-layouts  217 us (11%)
  matrix products  171 us (9%)
  blocking collectives  111 us (6%)
  other arithmetic  67.4 us (3%)
    psum x1, waiting for transfers between devices, body(): lax.psum((lax.psum_scatter(summed[0], 'fsdp', scatter_dimension=0, tiled=...  351 us
    reduce_scatter x2, waiting for transfers between devices, one_batch(): lax.psum_scatter(buffer, 'ctx', scatter_dimension=1, tiled=True)  226 us
    reduce_scatter x1, waiting for transfers between devices, body(): lax.psum_scatter(summed[9], 'fsdp', scatter_dimension=0, tiled=True)  192 us
    reduce_scatter x1, waiting for transfers between devices, body(): lax.psum_scatter(summed[11], 'fsdp', scatter_dimension=1, tiled=True)  191 us
    ppermute x30, waiting for transfers between devices, one_batch(): lax.ppermute(ring[-1], 'ctx', [(dev, (dev + 1) % 16) for dev in range(16)])  156 us
    reduce_scatter x1, waiting for transfers between devices, body(): lax.psum_scatter(summed[2], 'fsdp', scatter_dimension=0, tiled=True)  147 us
    unnamed x388, local copies, waits for them, and re-layouts  74.9 us
    dynamic_update_slice x8, local copies, waits for them, and re-layouts, key_grads(): lax.dynamic_update_slice_in_dim(running[1], joined_grad, number * size_k, 1)  66.3 us
  transfers between devices with their start and end apart: 41, of which 36 were waited for; matrix products, arithmetic and copies ran while one was open for 16% of the time, Pallas kernels for 0%

profile of v1, /device:TPU:0, one launch (start us, length us, event | category | flops | bytes accessed | tf_op | source)
XLA Modules:
  0.0 1962.9 jit_solution(13701163849002692858)
XLA Ops:
  29.0 63.8 %all-gather.13.cloned.1.call-done = bf16[1024,3072]{1,0:T(8,128)(2,1)} async-done(((bf16[512,3072]{1,0:T(8,128)(2,1)}), bf16[1024,3072]{1,0:T(8,128)(2,1)}) %all-gather.13.cloned.1.call-update) | async-done | bytes 6291472 | tf_op jit(solution)/shard_map/all_gather | solution.py:295
  100.6 9.6 collective-permute-done.15
  306.9 15.7 fusion.54
  322.6 11.9 copy.147
  334.5 16.3 while.122
  350.8 17.3 while.123
  370.2 11.8 copy.137
  382.0 16.2 while.120
  398.3 17.5 while.121
  461.8 10.5 while.126
  480.2 66.3 %while.127 = (s32[]{:T(128)}, f32[2,64,16,64]{1,3,2,0:T(8,128)}, f32[2,1024,2048]{2,1,0:T(8,128)}, bf16[2,1024,2048]{1,2,0:T(8,128)(2,1)}, s32[1024]{0:T(1024)S(...) while((s32[]{:T(128)}, f32[2,64,16,64]{1,3,2,0:T(8,128)}, ...), condition=%wide.region_37.41_spmd.clone, body=%wide.region_36.40_spmd.clone.sunk | while | flops 685277184 | bytes 136621136 | solution.py:226
  551.7 12.3 while.124
  564.0 9.1 broadcast.731.clone2.1
  573.1 66.9 %while.125 = (s32[]{:T(128)}, f32[2,64,16,64]{1,3,2,0:T(8,128)}, f32[2,1024,2048]{2,1,0:T(8,128)}, bf16[2,1024,2048]{1,2,0:T(8,128)(2,1)}, s32[1024]{0:T(1024)S(...) while((s32[]{:T(128)}, f32[2,64,16,64]{1,3,2,0:T(8,128)}, ...), condition=%wide.region_27.31_spmd.clone, body=%wide.region_26.30_spmd.clone.sunk | while | flops 685277184 | bytes 136621136 | solution.py:226
  589.8 8.9 copy.230
  661.9 9.9 bitcast_add_fusion
  675.6 46.0 %reduce-scatter.9.cloned.1.call-done = f32[2,64,2048]{2,1,0:T(8,128)} async-done(((f32[2,1024,2048]{2,1,0:T(8,128)}), f32[2,64,2048]{2,1,0:T(8,128)}) %reduce-scatter.9.cloned.1.call-update) | async-done | bytes 1048592 | tf_op jit(solution)/shard_map/reduce_scatter | solution.py:232
  723.0 180.3 %reduce-scatter.7.cloned.1.call-done = f32[2,64,2048]{2,1,0:T(8,128)} async-done(((f32[2,1024,2048]{2,1,0:T(8,128)}), f32[2,64,2048]{2,1,0:T(8,128)}) %reduce-scatter.7.cloned.1.call-update) | async-done | bytes 1048592 | tf_op jit(solution)/shard_map/reduce_scatter | solution.py:232
  913.5 46.0 %reduce-scatter.13.cloned.1.call-done = f32[1024,512]{1,0:T(8,128)} async-done(((f32[1024,1024]{1,0:T(8,128)}), f32[1024,512]{1,0:T(8,128)}) %reduce-scatter.13.cloned.1.call-update) | async-done | bytes 2097168 | tf_op jit(solution)/shard_map/reduce_scatter | solution.py:332
  959.5 191.6 %reduce-scatter.15.cloned.1.call-done = f32[512,4096]{1,0:T(8,128)} async-done(((f32[1024,4096]{1,0:T(8,128)}), f32[512,4096]{1,0:T(8,128)}) %reduce-scatter.15.cloned.1.call-update) | async-done | bytes 8388624 | tf_op jit(solution)/shard_map/reduce_scatter | solution.py:336
  1151.1 191.5 %reduce-scatter.17.cloned.1.call-done = f32[4096,512]{1,0:T(8,128)} async-done(((f32[4096,1024]{1,0:T(8,128)}), f32[4096,512]{1,0:T(8,128)}) %reduce-scatter.17.cloned.1.call-update) | async-done | bytes 8388624 | tf_op jit(solution)/shard_map/reduce_scatter | solution.py:338
  1342.5 146.7 %reduce-scatter.11.cloned.1.call-done = f32[512,3072]{1,0:T(8,128)} async-done(((f32[1024,3072]{1,0:T(8,128)}), f32[512,3072]{1,0:T(8,128)}) %reduce-scatter.11.cloned.1.call-update) | async-done | bytes 6291472 | tf_op jit(solution)/shard_map/reduce_scatter | solution.py:329
  1521.6 63.5 %all-reduce.9 = (f32[512]{0:T(512)}, f32[512]{0:T(512)}, f32[512]{0:T(512)}, f32[512]{0:T(512)}, f32[512]{0:T(512)}, /*index=5*/f32[512]{0:T(512)}, f32[512]{0:T(512)}, f32[2048]{0:T(1024)}, f32[512]{0:T(512)}) all-reduce(f32[512]{0:T(512)S(1)} %dynamic-slice.1, ...), channel_id=1, replica_groups=mesh['fsdp'=2,'ctx'=16] {'ctx'}, use_global_device_ids=true, to_apply=%region_44.48 | all-reduce | flops 6144 | bytes 49152 | tf_op jit(solution)/shard_map/psum | solution.py:325
  1587.7 350.7 %all-reduce.14.cloned.1.call-done = (f32[512,3072]{1,0:T(8,128)}, f32[1024,512]{1,0:T(8,128)}, f32[512,4096]{1,0:T(8,128)}, f32[4096,512]{1,0:T(8,128)}) async-done(((f32[512,3072]{1,0:T(8,128)}, f32[1024,512]{1,0:T(8,128)}, f32[512,4096]{1,0:T(8,128)}, f32[4096,512]{1,0:T(8,128)}), (f32[512,3072]{1,0:T(8,128)}, f32[1024,512]{1,0:T(8,128)}, f32[512,4096]{1,0:T(8,128)}, ...) | async-done | bytes 25165840 | tf_op jit(solution)/shard_map/psum | solution.py:325
  (769 shorter events, 586.7 us)
Async XLA Ops:
  7.2 85.5 %all-gather.13.cloned.1.call-start = ((), (), s32[]{:S(2)}) async-start(), calls=%async_computation.6 | async-start | bytes 9437184 | tf_op jit(solution)/shard_map/all_gather | solution.py:295
  8.0 410.2 %all-gather.15.cloned.1.call-start = ((), (), s32[]{:S(2)}) async-start(), calls=%async_computation.7 | async-start | bytes 3145728 | tf_op jit(solution)/shard_map/all_gather | solution.py:298
  8.7 414.8 %all-gather.17.cloned.1.call-start = ((), (), s32[]{:S(2)}) async-start(), calls=%async_computation.8 | async-start | bytes 12582912 | tf_op jit(solution)/shard_map/all_gather | solution.py:302
  9.5 423.1 %all-gather.19.cloned.1.call-start = ((), (), s32[]{:S(2)}) async-start(), calls=%async_computation.9 | async-start | bytes 12582912 | tf_op jit(solution)/shard_map/all_gather | solution.py:304
  98.8 11.4 collective-permute-start.15
  99.0 16.8 collective-permute-start
  144.1 12.0 collective-permute-start.19
  167.4 12.1 collective-permute-start.21
  179.5 11.3 collective-permute-start.22
  224.7 11.4 collective-permute-start.26
  230.4 11.4 collective-permute-start.11
  236.2 11.6 collective-permute-start.27
  236.2 485.5 %reduce-scatter.9.cloned.1.call-start = ((), (), s32[]{:S(2)}) async-start(), calls=%async_computation.11 | async-start | bytes 17825792 | tf_op jit(solution)/shard_map/reduce_scatter | solution.py:232
  241.8 11.6 collective-permute-start.12
  247.8 11.6 collective-permute-start.28
  253.5 36.9 %collective-permute-start.13 = (bf16[2,64,2048]{2,1,0:T(8,128)(2,1)}, bf16[2,64,2048]{2,1,0:T(8,128)(2,1)}, u32[]{:S(2)}, u32[]{:S(2)}) collective-permute-start(bf16[2,64,2048]{2,1,0:T(8,128)(2,1)} %collective-permute-done.12), channel_id=1, source_target_pairs={{0,1},{1,2},{2,3},{3,4},{4,5},{5,6},{6,7},{7,8},{8,9},{9,10},{10,1... | collective-permute-start | bytes 1572872 | tf_op jit(solution)/shard_map/ppermute | solution.py:88
  259.4 31.0 %collective-permute-start.29 = (bf16[2,64,2048]{2,1,0:T(8,128)(2,1)}, bf16[2,64,2048]{2,1,0:T(8,128)(2,1)}, u32[]{:S(2)}, u32[]{:S(2)}) collective-permute-start(bf16[2,64,2048]{2,1,0:T(8,128)(2,1)} %collective-permute-done.28), channel_id=1, source_target_pairs={{0,1},{1,2},{2,3},{3,4},{4,5},{5,6},{6,7},{7,8},{8,9},{9,10},{10,1... | collective-permute-start | bytes 1572872 | tf_op jit(solution)/shard_map/ppermute | solution.py:88
  290.3 11.6 collective-permute-start.14
  546.6 356.7 %reduce-scatter.7.cloned.1.call-start = ((), (), s32[]{:S(2)}) async-start(), calls=%async_computation.10 | async-start | bytes 17825792 | tf_op jit(solution)/shard_map/reduce_scatter | solution.py:232
  640.0 319.5 %reduce-scatter.13.cloned.1.call-start = ((), (), s32[]{:S(2)}) async-start(), calls=%async_computation.13 | async-start | bytes 6291456 | tf_op jit(solution)/shard_map/reduce_scatter | solution.py:332
  644.7 506.4 %reduce-scatter.15.cloned.1.call-start = ((), (), s32[]{:S(2)}) async-start(), calls=%async_computation.14 | async-start | bytes 25165824 | tf_op jit(solution)/shard_map/reduce_scatter | solution.py:336
  656.9 685.7 %reduce-scatter.17.cloned.1.call-start = ((), (), s32[]{:S(2)}) async-start(), calls=%async_computation.15 | async-start | bytes 25165824 | tf_op jit(solution)/shard_map/reduce_scatter | solution.py:338
  671.9 817.4 %reduce-scatter.11.cloned.1.call-start = ((), (), s32[]{:S(2)}) async-start(), calls=%async_computation.12 | async-start | bytes 18874368 | tf_op jit(solution)/shard_map/reduce_scatter | solution.py:329
  913.5 1025.0 %all-reduce.14.cloned.1.call-start = ((), (), s32[]{:S(2)}) async-start(), calls=%async_computation.16 | async-start | bytes 50331648 | tf_op jit(solution)/shard_map/psum | solution.py:325
  (189 other events, 5331.1 us)
Sparse Core Ops, SparseCore 0:
  9.6 83.0 all-gather.12
  94.3 33.1 all-gather.14
  129.0 103.9 all-gather.16
  236.3 104.4 all-gather.18
  546.6 174.9 reduce-scatter.8
  725.6 177.6 reduce-scatter.6
  906.2 53.3 reduce-scatter.12
  961.9 189.1 reduce-scatter.14
  1153.4 189.1 reduce-scatter.16
  1344.8 144.4 reduce-scatter.10
  1494.9 443.4 all-reduce.13
